TPU v7x, 256 devices: a whole 4x4x8 slice. The times are simulated.
256 devices in a mesh: fsdp: 64 (over z, x_hi, y), tp: 4 (over x_lo, core).
Axes of the slice: x: 4 (x_hi: 2, x_lo: 2; x = x_hi * 2 + x_lo), y: 4, z: 8, core: 2. Of those that a mesh axis runs over, the one named last changes fastest.
Arguments:
- tokens: bfloat16 [24576, 8192], P('fsdp', 'tp'), may hold values from -16 to 16
- cotangent: bfloat16 [24576, 1024], P('fsdp', 'tp'), may hold values from -6 to 6
- response_mask: int32 [24576], P('fsdp'), may hold values 0 or 1
- key_weight: bfloat16 [8192, 1024], P('fsdp', 'tp'), may hold values from -0.0625 to 0.0625
- new_hidden: bfloat16 [256, 8, 8192], P('fsdp'), may hold values from -6 to 6
- new_values: bfloat16 [256, 8, 1024], P('fsdp', None, 'tp'), may hold values from -6 to 6
- queries: bfloat16 [256, 8, 8192], P('fsdp', None, 'tp'), may hold values from -16 to 16, as said below
- cache_keys: bfloat16 [256, 2048, 1024], P('fsdp', None, 'tp'), may hold values from -16 to 16, as said below
- cache_values: bfloat16 [256, 2048, 1024], P('fsdp', None, 'tp'), may hold values from -6 to 6
- cache_lengths: int32 [256], P('fsdp'), may hold values from 1 to 2048, as said below
Outputs:
- grad_inputs: bfloat16 [24576, 8192], P('fsdp', 'tp')
- learner_weight: bfloat16 [8192, 1024], P('fsdp', 'tp')
- new_keys: bfloat16 [256, 8, 1024], P('fsdp', None, 'tp')
- context: bfloat16 [256, 8, 8192], P('fsdp', None, 'tp')
Inputs may be any that keep to these rules, and one draw needn't show every extreme that they name: `queries`: queries of the decoded tokens, already rotated. `cache_keys`: cached keys, already rotated. `cache_lengths`: some request has exactly 2048 valid slots.
All inputs are finite; a program needn't handle non-finite values. No bound on the sum of `response_mask` on one device may be relied on, other than what follows from the above.
Results may differ from a plain program's by a relative error of at most 0.0095.
Values may be sent and summed in bfloat16 or wider, within the bound.
No kernel may reach another device: no remote copies, remote signals or barrier semaphores. Data moves between devices by JAX's collectives and lax.ppermute only.
A program may use at most 128 MiB of HBM per device.

v0:
```python
import math
import jax
import jax.numpy as jnp
from jax import lax
from jax.sharding import PartitionSpec as P

D = 8192
HD = 128
ROPE_BASE = 1000000.0


def rope_rotate(keys, positions):
    half = keys.shape[-1] // 2
    freq = ROPE_BASE ** (-jnp.arange(half, dtype=jnp.float32) * (2.0 / keys.shape[-1]))
    angle = positions.astype(jnp.float32)[..., None] * freq
    cosine = jnp.cos(angle)[..., None, :]
    sine = jnp.sin(angle)[..., None, :]
    first = keys[..., :half]
    second = keys[..., half:]
    return jnp.concatenate(
        [first * cosine - second * sine, second * cosine + first * sine], axis=-1
    )


def attend(queries, cache_keys, cache_values, new_keys, new_values, lengths):
    count, steps = (queries.shape[0], queries.shape[1])
    slots = cache_keys.shape[1]
    groups = cache_keys.shape[2] // HD
    share = queries.shape[2] // cache_keys.shape[2]
    inv = 1.0 / math.sqrt(HD)
    query = queries.reshape(count, steps, groups, share, HD)
    old_keys = cache_keys.reshape(count, slots, groups, HD)
    old_values = cache_values.reshape(count, slots, groups, HD)
    fresh_keys = new_keys.reshape(count, steps, groups, HD)
    fresh_values = new_values.reshape(count, steps, groups, HD)
    cache_scores = (
        jnp.einsum("rsjgd,rcjd->rsjgc", query, old_keys, preferred_element_type=jnp.float32) * inv
    )
    fresh_scores = (
        jnp.einsum("rsjgd,rtjd->rsjgt", query, fresh_keys, preferred_element_type=jnp.float32) * inv
    )
    cache_valid = jnp.arange(slots, dtype=jnp.int32)[None, :] < lengths[:, None]
    step_ids = jnp.arange(steps, dtype=jnp.int32)
    fresh_valid = step_ids[None, :] <= step_ids[:, None]
    cache_scores = jnp.where(cache_valid[:, None, None, None, :], cache_scores, -jnp.inf)
    fresh_scores = jnp.where(fresh_valid[None, :, None, None, :], fresh_scores, -jnp.inf)
    top = jnp.maximum(jnp.max(cache_scores, axis=-1), jnp.max(fresh_scores, axis=-1))[..., None]
    cache_exp = jnp.exp(cache_scores - top)
    fresh_exp = jnp.exp(fresh_scores - top)
    total = jnp.sum(cache_exp, axis=-1, keepdims=True) + jnp.sum(fresh_exp, axis=-1, keepdims=True)
    cache_weights = (cache_exp / total).astype(jnp.bfloat16)
    fresh_weights = (fresh_exp / total).astype(jnp.bfloat16)
    mixed = jnp.einsum(
        "rsjgc,rcjd->rsjgd", cache_weights, old_values, preferred_element_type=jnp.float32
    )
    mixed = mixed + jnp.einsum(
        "rsjgt,rtjd->rsjgd", fresh_weights, fresh_values, preferred_element_type=jnp.float32
    )
    return mixed.reshape(count, steps, groups * share * HD).astype(jnp.bfloat16)


def per_device(
    tokens,
    cotangent,
    response_mask,
    key_weight,
    new_hidden,
    new_values,
    queries,
    cache_keys,
    cache_values,
    cache_lengths,
):
    masked = cotangent * response_mask[:, None].astype(jnp.bfloat16)
    rows = key_weight.shape[0]
    scale = 1.0 / math.sqrt(D * tokens.shape[0] * lax.axis_size("fsdp"))
    full_weight = lax.all_gather(key_weight, "fsdp", axis=0, tiled=True)
    whole = lax.all_gather(tokens, "tp", axis=1, tiled=True)
    partial_value = jnp.einsum("tc,tk->ck", whole, masked, preferred_element_type=jnp.float32)
    terms = jnp.einsum("tk,ck->tc", masked, full_weight, preferred_element_type=jnp.float32)
    grad_inputs = lax.psum_scatter(
        terms.astype(jnp.bfloat16), "tp", scatter_dimension=1, tiled=True
    )
    grad = lax.psum(partial_value, "fsdp")
    rollout_weight = (full_weight.astype(jnp.float32) - grad * scale).astype(jnp.bfloat16)
    learner_weight = lax.dynamic_slice_in_dim(
        rollout_weight, lax.axis_index("fsdp") * rows, rows, 0
    )
    requests, steps = (new_hidden.shape[0], new_hidden.shape[1])
    raw = jnp.einsum("rsd,dk->rsk", new_hidden, rollout_weight, preferred_element_type=jnp.float32)
    local_width = raw.shape[2]
    positions = cache_lengths[:, None] + jnp.arange(steps, dtype=jnp.int32)[None, :]
    rotated = rope_rotate(raw.reshape(requests, steps, local_width // HD, HD), positions)
    new_keys = rotated.astype(jnp.bfloat16).reshape(requests, steps, local_width)
    context = attend(queries, cache_keys, cache_values, new_keys, new_values, cache_lengths)
    return (grad_inputs, learner_weight, new_keys, context)


def solution(mesh):
    placed = (
        P("fsdp", "tp"),
        P("fsdp", "tp"),
        P("fsdp"),
        P("fsdp", "tp"),
        P("fsdp", None, None),
        P("fsdp", None, "tp"),
        P("fsdp", None, "tp"),
        P("fsdp", None, "tp"),
        P("fsdp", None, "tp"),
        P("fsdp"),
    )
    return jax.shard_map(
        per_device,
        mesh=mesh,
        in_specs=placed,
        out_specs=(P("fsdp", "tp"), P("fsdp", "tp"), P("fsdp", None, "tp"), P("fsdp", None, "tp")),
        check_vma=False,
    )
```

profile of v0, /device:TPU:1, one launch (start us, length us, event | category | flops | bytes accessed | tf_op | source)
XLA Modules:
  0.0 1011.2 jit_solution(13662762769809048783)
XLA Ops:
  7.2 0.0 copy-start
  7.2 0.0 all-gather.5.cloned.1.call-start
  7.2 0.7 all-gather.5.cloned.1.call-update
  7.9 0.0 all-gather.3.cloned.1.call-start
  8.0 1.6 copy.22
  9.5 0.0 all-gather.3.cloned.1.call-update
  9.6 0.0 all-reduce.2.cloned.1.call-start
  9.6 0.7 convert_element_type.42
  10.3 70.2 %all-gather.5.cloned.1.call-done = bf16[384,8192]{1,0:T(8,128)(2,1)} async-done(((bf16[384,2048]{1,0:T(8,128)(2,1)}), bf16[384,8192]{1,0:T(8,128)(2,1)}) %all-gather.5.cloned.1.call-update) | async-done | bytes 6291472 | tf_op jit(solution)/shard_map/all_gather | solution.py:78
  80.5 8.6 convolution_bitcast_fusion
  89.1 0.0 copy-start.4
  89.1 0.0 all-reduce.2.cloned.1.call-update
  89.1 0.0 reduce-scatter.2.cloned.1.call-start
  89.2 120.4 %all-gather.3.cloned.1.call-done = bf16[8192,256]{0,1:T(8,128)(2,1)} async-done(((bf16[128,256]{0,1:T(8,128)(2,1)}), bf16[8192,256]{0,1:T(8,128)(2,1)}) %all-gather.3.cloned.1.call-update) | async-done | bytes 4194320 | tf_op jit(solution)/shard_map/all_gather | solution.py:77
  209.6 0.0 copy-done.4
  209.6 6.7 convolution_convert_fusion
  216.3 0.0 reduce-scatter.2.cloned.1.call-update
  216.3 6.9 reshape.100
  223.2 0.0 copy-start.6
  223.2 0.0 copy-start.5
  223.2 7.0 reshape.102
  230.3 0.0 copy-done.6
  230.3 0.1 add_convert_fusion
  230.4 0.1 multiply_cosine_fusion
  230.5 0.1 iota_compare_fusion
  230.6 0.0 copy-done.5
  230.6 5.7 bitcast_reduce_fusion
  236.3 656.1 %all-reduce.2.cloned.1.call-done = f32[8192,256]{0,1:T(8,128)} async-done(((f32[8192,256]{0,1:T(8,128)}), f32[8192,256]{0,1:T(8,128)}) %all-reduce.2.cloned.1.call-update) | async-done | bytes 8388624 | tf_op jit(solution)/shard_map/psum | solution.py:84
  892.5 5.8 subtract_convert_fusion
  898.3 0.0 copy-done
  898.3 0.0 copy-start.1
  898.3 0.0 copy-start.3
  898.3 1.3 fusion.17
  899.6 0.0 copy-start.2
  899.6 0.1 multiply_subtract_fusion
  899.7 0.7 fusion.33
  900.5 0.0 copy-done.1
  900.5 0.1 fusion.20
  900.6 1.4 copy-done.3
  902.0 1.0 fusion.7
  903.0 0.3 copy-done.2
  903.2 0.0 copy-start.7
  903.2 1.7 fusion
  905.0 0.0 copy-done.7
  905.0 0.3 fusion.16
  905.3 0.7 convert_element_type.53
  906.0 0.8 constant_dynamic-slice_fusion
  906.8 0.7 copy.30
  907.6 0.7 fusion.34
  908.3 96.4 %reduce-scatter.2.cloned.1.call-done = bf16[384,2048]{1,0:T(8,128)(2,1)} async-done(((bf16[384,8192]{1,0:T(8,128)(2,1)}), bf16[384,2048]{1,0:T(8,128)(2,1)}) %reduce-scatter.2.cloned.1.call-update) | async-done | bytes 1572880 | tf_op jit(solution)/shard_map/reduce_scatter | solution.py:81
  (5 shorter events, 0.1 us)
Async XLA Ops:
  7.2 891.1 %copy-start = (bf16[4,8,8192]{2,1,0:T(8,128)(2,1)S(1)}, bf16[4,8,8192]{2,1,0:T(8,128)(2,1)}, u32[]{:S(2)}) copy-start(bf16[4,8,8192]{2,1,0:T(8,128)(2,1)} %param.14) | copy-start | bytes 1572868
  7.2 73.3 %all-gather.5.cloned.1.call-start = ((), (), s32[]{:S(2)}) async-start(), calls=%async_computation.3 | async-start | bytes 7864320 | tf_op jit(solution)/shard_map/all_gather | solution.py:78
  7.9 201.7 %all-gather.3.cloned.1.call-start = ((), (), s32[]{:S(2)}) async-start(), calls=%async_computation.1 | async-start | bytes 4259840 | tf_op jit(solution)/shard_map/all_gather | solution.py:77
  9.6 882.9 %all-reduce.2.cloned.1.call-start = ((), (), s32[]{:S(2)}) async-start(), calls=%async_computation.4 | async-start | bytes 16777216 | tf_op jit(solution)/shard_map/psum | solution.py:84
  89.1 120.5 %copy-start.4 = (bf16[384,256]{1,0:T(8,128)(2,1)S(1)}, bf16[384,256]{1,0:T(8,128)(2,1)}, u32[]{:S(2)}) copy-start(bf16[384,256]{1,0:T(8,128)(2,1)} %param.11) | copy-start | bytes 589828
  89.1 915.5 %reduce-scatter.2.cloned.1.call-start = ((), (), s32[]{:S(2)}) async-start(), calls=%async_computation.2 | async-start | bytes 7864320 | tf_op jit(solution)/shard_map/reduce_scatter | solution.py:81
  223.2 7.1 copy-start.6
  223.2 7.4 copy-start.5
  898.3 2.2 copy-start.1
  898.3 3.7 copy-start.3
  899.6 3.6 copy-start.2
  903.2 1.7 copy-start.7
Sparse Core Ops, SparseCore 0:
  9.8 70.6 all-gather.4
  84.5 125.0 all-gather.2
  212.3 680.1 all-reduce.1
  895.5 109.1 reduce-scatter.1
where the time goes:
time: 1010 us
  waiting for transfers between devices  944 us (93%)
  matrix products  25 us (2%)
  local copies, waits for them, and re-layouts  19.5 us (2%)
  between operations  13.9 us (1%)
    psum x1, waiting for transfers between devices, per_device(): grad = lax.psum(partial_value, 'fsdp')  656 us
    all_gather x1, waiting for transfers between devices, per_device(): full_weight = lax.all_gather(key_weight, 'fsdp', axis=0, tiled=True)  120 us
    reduce_scatter x1, waiting for transfers between devices, per_device(): lax.psum_scatter(terms.astype(jnp.bfloat16), 'tp', scatter_dimension=1, t...  96.4 us
    all_gather x1, waiting for transfers between devices, per_device(): whole = lax.all_gather(tokens, 'tp', axis=1, tiled=True)  70.2 us
  transfers between devices with their start and end apart: 4, of which 4 were waited for; matrix products, arithmetic and copies ran while one was open for 5% of the time, Pallas kernels for 0%

commit v1 on v0

--- a/solution.py
+++ b/solution.py
@@ -75,7 +75,10 @@
     rows = key_weight.shape[0]
     scale = 1.0 / math.sqrt(D * tokens.shape[0] * lax.axis_size("fsdp"))
     full_weight = lax.all_gather(key_weight, "fsdp", axis=0, tiled=True)
-    whole = lax.all_gather(tokens, "tp", axis=1, tiled=True)
+    reached = lax.axis_size("tp")
+    x_next = jnp.stack(reached * [tokens])
+    state_now = lax.all_to_all(x_next, "tp", split_axis=0, concat_axis=0)
+    whole = jnp.concatenate(state_now, axis=1)
     partial_value = jnp.einsum("tc,tk->ck", whole, masked, preferred_element_type=jnp.float32)
     terms = jnp.einsum("tk,ck->tc", masked, full_weight, preferred_element_type=jnp.float32)
     grad_inputs = lax.psum_scatter(

time: 1010 us -> 945 us (0.936)
  waiting for transfers between devices: 944 us -> 864 us
    all_gather x1, waiting for transfers between devices: 120 us -> 39.3 us  [per_device(): full_weight = lax.all_gather(key_weight, 'fsdp', axis=0, tiled=True)]
    all_to_all x0 -> x1, waiting for transfers between devices: none -> 70.4 us  [per_device(): state_now = lax.all_to_all(x_next, 'tp', split_axis=0, concat_axis=0)]
    all_gather x1 -> x0, waiting for transfers between devices: 70.2 us -> none  [per_device(): whole = lax.all_gather(tokens, 'tp', axis=1, tiled=True)]
  transfers between devices with their start and end apart: 4 -> 4, of which waited for: 4 -> 4; matrix products, arithmetic and copies ran while one was open for 5% -> 6% of each run, Pallas kernels for 0% -> 0%
where the time goes in v1:
time: 945 us; the launch traced here: 944 us
  waiting for transfers between devices  864 us (91%)
  matrix products  25.1 us (3%)
  local copies, waits for them, and re-layouts  24.6 us (3%)
  between operations  13.9 us (1%)
    psum x1, waiting for transfers between devices, per_device(): grad = lax.psum(partial_value, 'fsdp')  658 us
    reduce_scatter x1, waiting for transfers between devices, per_device(): lax.psum_scatter(terms.astype(jnp.bfloat16), 'tp', scatter_dimension=1, t...  96.5 us
    all_to_all x1, waiting for transfers between devices, per_device(): state_now = lax.all_to_all(x_next, 'tp', split_axis=0, concat_axis=0)  70.4 us
    all_gather x1, waiting for transfers between devices, per_device(): full_weight = lax.all_gather(key_weight, 'fsdp', axis=0, tiled=True)  39.3 us
  transfers between devices with their start and end apart: 4, of which 4 were waited for; matrix products, arithmetic and copies ran while one was open for 6% of the time, Pallas kernels for 0%

profile of v1, /device:TPU:1, one launch (start us, length us, event | category | flops | bytes accessed | tf_op | source)
XLA Modules:
  0.0 944.4 jit_solution(4135705340501004490)
XLA Ops:
  7.2 0.0 copy-start
  7.2 0.0 all-gather.2.cloned.1.call-start
  7.2 1.6 copy.22
  8.8 0.0 all-gather.2.cloned.1.call-update
  8.9 1.9 copy.23
  10.8 3.2 stack.2
  13.9 0.0 copy-start.7
  13.9 0.0 copy-start.4
  13.9 8.5 all-to-all-start
  22.5 0.0 all-reduce.2.cloned.1.call-start
  22.5 0.0 copy-done.7
  22.5 70.4 %all-to-all-done = bf16[4,384,2048]{1,2,0:T(8,128)(2,1)} async-done(((bf16[4,384,2048]{1,2,0:T(8,128)(2,1)}), bf16[4,384,2048]{1,2,0:T(8,128)(2,1)}, u32[]{:S(2)}, u32[]{:S(2)}) %all-to-all-start) | async-done | bytes 6291488 | tf_op jit(solution)/shard_map/all_to_all | solution.py:80
  92.9 0.0 copy-done.4
  92.9 8.6 convolution_bitcast_fusion
  101.5 0.0 all-reduce.2.cloned.1.call-update
  101.6 0.2 reduce-scatter.2.cloned.1.call-start
  101.8 39.3 %all-gather.2.cloned.1.call-done = bf16[8192,256]{0,1:T(8,128)(2,1)} async-done(((bf16[128,256]{0,1:T(8,128)(2,1)}), bf16[8192,256]{0,1:T(8,128)(2,1)}) %all-gather.2.cloned.1.call-update) | async-done | bytes 4194320 | tf_op jit(solution)/shard_map/all_gather | solution.py:77
  141.1 6.7 convolution_convert_fusion
  147.8 0.0 reduce-scatter.2.cloned.1.call-update
  147.8 6.9 reshape.110
  154.7 0.0 copy-start.6
  154.7 0.0 copy-start.5
  154.7 7.0 reshape.112
  161.7 0.0 copy-done.6
  161.7 0.1 add_convert_fusion
  161.8 0.1 multiply_cosine_fusion
  161.9 0.1 iota_compare_fusion
  162.0 0.0 copy-done.5
  162.0 5.7 bitcast_reduce_fusion
  167.7 657.8 %all-reduce.2.cloned.1.call-done = f32[8192,256]{0,1:T(8,128)} async-done(((f32[8192,256]{0,1:T(8,128)}), f32[8192,256]{0,1:T(8,128)}) %all-reduce.2.cloned.1.call-update) | async-done | bytes 8388624 | tf_op jit(solution)/shard_map/psum | solution.py:87
  825.5 5.8 subtract_convert_fusion
  831.3 0.0 copy-done
  831.3 0.0 copy-start.1
  831.3 0.0 copy-start.3
  831.3 1.3 fusion.17
  832.7 0.0 copy-start.2
  832.7 0.1 multiply_subtract_fusion
  832.8 0.7 fusion.33
  833.5 0.0 copy-done.1
  833.5 0.1 fusion.20
  833.6 1.4 copy-done.3
  835.0 1.0 fusion.7
  836.0 0.3 copy-done.2
  836.3 0.0 copy-start.8
  836.3 1.7 fusion
  838.0 0.0 copy-done.8
  838.0 0.3 fusion.16
  838.3 0.7 convert_element_type.53
  839.0 0.8 constant_dynamic-slice_fusion
  839.9 0.7 copy.31
  840.6 0.7 fusion.34
  841.3 96.5 %reduce-scatter.2.cloned.1.call-done = bf16[384,2048]{1,0:T(8,128)(2,1)} async-done(((bf16[384,8192]{1,0:T(8,128)(2,1)}), bf16[384,2048]{1,0:T(8,128)(2,1)}) %reduce-scatter.2.cloned.1.call-update) | async-done | bytes 1572880 | tf_op jit(solution)/shard_map/reduce_scatter | solution.py:84
  (6 shorter events, 0.1 us)
Async XLA Ops:
  7.2 824.1 %copy-start = (bf16[4,8,8192]{2,1,0:T(8,128)(2,1)S(1)}, bf16[4,8,8192]{2,1,0:T(8,128)(2,1)}, u32[]{:S(2)}) copy-start(bf16[4,8,8192]{2,1,0:T(8,128)(2,1)} %param.14) | copy-start | bytes 1572868
  7.2 133.9 %all-gather.2.cloned.1.call-start = ((), (), s32[]{:S(2)}) async-start(), calls=%async_computation.2 | async-start | bytes 4259840 | tf_op jit(solution)/shard_map/all_gather | solution.py:77
  13.9 8.5 copy-start.7
  13.9 79.0 %copy-start.4 = (bf16[384,256]{1,0:T(8,128)(2,1)S(1)}, bf16[384,256]{1,0:T(8,128)(2,1)}, u32[]{:S(2)}) copy-start(bf16[384,256]{1,0:T(8,128)(2,1)} %param.11) | copy-start | bytes 589828
  13.9 79.0 %all-to-all-start = ((bf16[4,384,2048]{1,2,0:T(8,128)(2,1)}), bf16[4,384,2048]{1,2,0:T(8,128)(2,1)}, u32[]{:S(2)}, u32[]{:S(2)}) async-start(bf16[4,384,2048]{1,2,0:T(8,128)(2,1)} %stack.2), calls=%async_computation.1 | async-start | bytes 12582912 | tf_op jit(solution)/shard_map/all_to_all | solution.py:80
  22.5 803.1 %all-reduce.2.cloned.1.call-start = ((), (), s32[]{:S(2)}) async-start(), calls=%async_computation.4 | async-start | bytes 16777216 | tf_op jit(solution)/shard_map/psum | solution.py:87
  101.6 836.3 %reduce-scatter.2.cloned.1.call-start = ((), (), s32[]{:S(2)}) async-start(), calls=%async_computation.3 | async-start | bytes 7864320 | tf_op jit(solution)/shard_map/reduce_scatter | solution.py:84
  154.7 7.0 copy-start.6
  154.7 7.3 copy-start.5
  831.3 2.2 copy-start.1
  831.3 3.7 copy-start.3
  832.7 3.6 copy-start.2
  836.3 1.7 copy-start.8
Sparse Core Ops, SparseCore 0:
  12.0 129.0 all-gather.1
  143.7 681.7 all-reduce.1
  828.7 109.1 reduce-scatter.1
